TPU v7x, 256 devices: a whole 4x4x8 slice. The times are simulated.
256 devices in a mesh: grp: 8 (over y, core), sub: 32 (over x, z).
Axes of the slice: x: 4, y: 4, z: 8, core: 2. Of those that a mesh axis runs over, the one named last changes fastest.
Arguments:
- cluster_pos: float32 [3, 4096], P(None, 'sub'), may hold values from -3 to 3
- cluster_vel: float32 [3, 4096], P(None, 'sub'), may hold values from -15 to 15
- cluster_mass: float32 [4096], P('sub'), may hold values from 3 to 60
- galaxy_pos: float32 [3, 131072], P(None, ('grp', 'sub')), may hold values from -1 to 7
- galaxy_vel: float32 [3, 131072], P(None, ('grp', 'sub')), may hold values from -3 to 3
- galaxy_kind: int32 [131072], P(('grp', 'sub')), may hold values from 0 to 3
- species_mass: float32 [4], replicated, may hold values from 10 to 80
Outputs:
- cluster_pos_out: float32 [3, 4096], P(None, 'sub')
- cluster_vel_out: float32 [3, 4096], P(None, 'sub')
- galaxy_pos_out: float32 [3, 131072], P(None, ('grp', 'sub'))
- galaxy_vel_out: float32 [3, 131072], P(None, ('grp', 'sub'))
All inputs are finite; a program needn't handle non-finite values.
Results may differ from a plain program's by a relative error of at most 0.0003.
Values sent between devices are 32-bit elements; how exact they have to be, the bound alone decides.
A program may use at most 64 MiB of HBM per device.

v0:
```python
import jax
import jax.numpy as jnp
from jax import lax
from jax.sharding import PartitionSpec as P

SUBSTEPS = 8
step_time = 0.5
bridge_soft = 0.01
cluster_soft = 0.0025
tile_limit = 524288


def pick_block(target_count, source_count):
    tile_size = target_count
    while tile_size > 1 and (
        tile_size * source_count > tile_limit or target_count % tile_size != 0
    ):
        tile_size = tile_size // 2
    return tile_size


def field(targets, sources, masses, soften):
    target_count = targets.shape[1]
    tile_size = pick_block(target_count, sources.shape[1])

    def field_one_tile(target_tile):
        separation = sources[:, None, :] - target_tile[:, :, None]
        distance = jnp.sum(separation * separation, axis=0) + soften
        inverse = lax.rsqrt(distance)
        weight = masses[None, :] * inverse * inverse * inverse
        return jnp.sum(separation * weight[None], axis=2)

    stacked = targets.reshape(3, target_count // tile_size, tile_size).transpose(1, 0, 2)
    result = lax.map(field_one_tile, stacked)
    return result.transpose(1, 0, 2).reshape(3, target_count)


def rates(target_pos, target_vel, source_pos, source_vel, masses, soften):
    target_count = target_pos.shape[1]
    tile_size = pick_block(target_count, source_pos.shape[1])

    def rates_one_tile(target_tile):
        separation = source_pos[:, None, :] - target_tile[:3, :, None]
        closing = source_vel[:, None, :] - target_tile[3:, :, None]
        distance = jnp.sum(separation * separation, axis=0) + soften
        inverse = lax.rsqrt(distance)
        weight = masses[None, :] * inverse * inverse * inverse
        radial = 3.0 * jnp.sum(separation * closing, axis=0) / distance
        acceleration = jnp.sum(separation * weight[None], axis=2)
        jerk_rate = jnp.sum((closing - radial[None] * separation) * weight[None], axis=2)
        return jnp.concatenate([acceleration, jerk_rate], axis=0)

    stacked = jnp.concatenate([target_pos, target_vel], axis=0)
    stacked = stacked.reshape(6, target_count // tile_size, tile_size).transpose(1, 0, 2)
    result = lax.map(rates_one_tile, stacked)
    return result.transpose(1, 0, 2).reshape(6, target_count)


def local(
    cluster_pos, cluster_vel, cluster_mass, galaxy_pos, galaxy_vel, galaxy_kind, species_mass
):
    star_count = cluster_pos.shape[1]
    member_count = lax.axis_size("sub")
    group_count = lax.axis_size("grp")
    total_stars = star_count * member_count
    total_bodies = galaxy_pos.shape[1] * member_count * group_count
    star_mass = cluster_mass / total_stars
    species = jnp.arange(species_mass.shape[0], dtype=jnp.int32)
    body_mass = (
        jnp.sum(
            jnp.where(galaxy_kind[None, :] == species[:, None], species_mass[:, None], 0.0), axis=0
        )
        / total_bodies
    )
    half_step = step_time / 2.0

    def kick(star_positions, body_positions):
        stacked = jnp.concatenate([star_positions, star_mass[None, :]], axis=0)
        gathered = lax.all_gather(stacked, "sub", axis=1, tiled=True)
        galaxy_push = field(body_positions, gathered[:3], gathered[3], bridge_soft)
        partial_value = field(gathered[:3], body_positions, body_mass, bridge_soft)
        summed = lax.psum(partial_value, ("grp", "sub"))
        cluster_pull = lax.dynamic_slice_in_dim(
            summed, lax.axis_index("sub") * star_count, star_count, 1
        )
        return (cluster_pull, galaxy_push)

    def evaluate(guess_pos, guess_vel):
        sources = jnp.concatenate([guess_pos, guess_vel, star_mass[None, :]], axis=0)
        target_pos, target_vel = (guess_pos, guess_vel)
        source_piece = lax.all_gather(sources, "sub", axis=1, tiled=True)
        result = rates(
            target_pos,
            target_vel,
            source_piece[:3],
            source_piece[3:6],
            source_piece[6],
            cluster_soft,
        )
        return (result[:3], result[3:])

    first_pull, first_push = kick(cluster_pos, galaxy_pos)
    star_vel = cluster_vel + half_step * first_pull
    body_vel = galaxy_vel + half_step * first_push
    body_pos = galaxy_pos + step_time * body_vel
    substep_time = step_time / SUBSTEPS
    positions, velocity = (cluster_pos, star_vel)
    acceleration, jerk_rate = evaluate(positions, velocity)
    for substep in range(SUBSTEPS):
        guess_pos = positions + substep_time * (
            velocity + substep_time * (acceleration / 2.0 + substep_time * jerk_rate / 6.0)
        )
        guess_vel = velocity + substep_time * (acceleration + substep_time * jerk_rate / 2.0)
        new_acc, new_jerk = evaluate(guess_pos, guess_vel)
        new_vel = (
            velocity
            + substep_time / 2.0 * (acceleration + new_acc)
            + substep_time * substep_time / 12.0 * (jerk_rate - new_jerk)
        )
        new_pos = (
            positions
            + substep_time / 2.0 * (velocity + new_vel)
            + substep_time * substep_time / 12.0 * (acceleration - new_acc)
        )
        positions, velocity, acceleration, jerk_rate = (new_pos, new_vel, new_acc, new_jerk)
    second_pull, second_push = kick(positions, body_pos)
    return (
        positions,
        velocity + half_step * second_pull,
        body_pos,
        body_vel + half_step * second_push,
    )


def solution(mesh):
    return jax.shard_map(
        local,
        mesh=mesh,
        in_specs=(
            P(None, "sub"),
            P(None, "sub"),
            P("sub"),
            P(None, ("grp", "sub")),
            P(None, ("grp", "sub")),
            P(("grp", "sub")),
            P(),
        ),
        out_specs=(
            P(None, "sub"),
            P(None, "sub"),
            P(None, ("grp", "sub")),
            P(None, ("grp", "sub")),
        ),
        check_vma=False,
    )
```

profile of v0, /device:TPU:1, one launch (start us, length us, event | category | flops | bytes accessed | tf_op | source)
XLA Modules:
  0.0 715.4 jit_solution(4176489332510097580)
XLA Ops:
  2.0 40.5 %all_gather.33 = f32[4,4096]{1,0:T(4,128)S(1)} all-gather(f32[4,128]{1,0:T(4,128)S(1)} %pad_maximum_fusion.10), channel_id=1, replica_groups=mesh['grp'=8,'sub'=32] {'sub'}, dimensions={1}, use_global_device_ids=true | all-gather | bytes 67584 | tf_op jit(solution)/shard_map/all_gather | solution.py:79
  43.3 14.5 %while.8 = (s32[]{:T(128)}, f32[4,3,1024]{2,1,0:T(4,128)S(1)}, f32[3,512]{1,0:T(4,128)}, f32[4,3,1024]{2,1,0:T(4,128)S(1)}, f32[512]{0:T(512)S(1)}, /*index=5*/s32[]{:T(128)}) while((s32[]{:T(128)}, f32[4,3,1024]{2,1,0:T(4,128)S(1)}, f32[3,512]{1,0:T(4,128)}, f32[4,3,1024]{2,1,0:T(4,128)S(1)}, f32[512]{0:T(512)S(1)}, ...), condition=%wide.region_4.5_spmd, body=%wide.region_1.4_spmd.sunk | while | flops 11006978 | bytes 8521833 | solution.py:34
  43.3 1.6 fusion.70
  45.6 1.2 fusion.71
  46.9 1.6 fusion.70
  49.3 1.2 fusion.71
  50.5 1.6 fusion.70
  52.9 1.2 fusion.71
  54.2 1.6 fusion.70
  56.5 1.2 fusion.71
  57.8 87.6 %psum.14 = f32[3,4096]{1,0:T(4,128)S(1)} all-reduce(f32[3,4096]{1,0:T(4,128)S(1)} %bitcast.93), channel_id=1, replica_groups=mesh['grp'=8,'sub'=32] {'grp','sub'}, use_global_device_ids=true, to_apply=%region_5.6 | all-reduce | flops 12288 | bytes 98304 | tf_op jit(solution)/shard_map/psum | solution.py:82
  145.4 31.0 %all_gather.34 = f32[7,4096]{1,0:T(8,128)S(1)} all-gather(f32[7,128]{1,0:T(8,128)S(1)} %pad_maximum_fusion.8), channel_id=1, replica_groups=mesh['grp'=8,'sub'=32] {'sub'}, dimensions={1}, use_global_device_ids=true | all-gather | bytes 118272 | tf_op jit(solution)/shard_map/all_gather | solution.py:91
  176.4 1.9 fusion.26
  179.0 2.1 fusion.27
  181.2 32.3 %all_gather.35 = f32[7,4096]{1,0:T(8,128)S(1)} all-gather(f32[7,128]{1,0:T(8,128)S(1)} %pad_maximum_fusion.7), channel_id=1, replica_groups=mesh['grp'=8,'sub'=32] {'sub'}, dimensions={1}, use_global_device_ids=true | all-gather | bytes 118272 | tf_op jit(solution)/shard_map/all_gather | solution.py:91
  213.5 2.0 fusion.31
  216.2 2.2 fusion.11
  218.4 31.8 %all_gather.36 = f32[7,4096]{1,0:T(8,128)S(1)} all-gather(f32[7,128]{1,0:T(8,128)S(1)} %pad_maximum_fusion.6), channel_id=1, replica_groups=mesh['grp'=8,'sub'=32] {'sub'}, dimensions={1}, use_global_device_ids=true | all-gather | bytes 118272 | tf_op jit(solution)/shard_map/all_gather | solution.py:91
  250.2 2.0 fusion.34
  252.9 2.2 fusion.13
  255.1 33.7 %all_gather.37 = f32[7,4096]{1,0:T(8,128)S(1)} all-gather(f32[7,128]{1,0:T(8,128)S(1)} %pad_maximum_fusion.5), channel_id=1, replica_groups=mesh['grp'=8,'sub'=32] {'sub'}, dimensions={1}, use_global_device_ids=true | all-gather | bytes 118272 | tf_op jit(solution)/shard_map/all_gather | solution.py:91
  288.9 2.0 fusion.37
  291.5 2.2 fusion.15
  293.7 30.9 %all_gather.38 = f32[7,4096]{1,0:T(8,128)S(1)} all-gather(f32[7,128]{1,0:T(8,128)S(1)} %pad_maximum_fusion.4), channel_id=1, replica_groups=mesh['grp'=8,'sub'=32] {'sub'}, dimensions={1}, use_global_device_ids=true | all-gather | bytes 118272 | tf_op jit(solution)/shard_map/all_gather | solution.py:91
  324.6 2.0 fusion.40
  327.3 2.2 fusion.17
  329.5 33.5 %all_gather.39 = f32[7,4096]{1,0:T(8,128)S(1)} all-gather(f32[7,128]{1,0:T(8,128)S(1)} %pad_maximum_fusion.3), channel_id=1, replica_groups=mesh['grp'=8,'sub'=32] {'sub'}, dimensions={1}, use_global_device_ids=true | all-gather | bytes 118272 | tf_op jit(solution)/shard_map/all_gather | solution.py:91
  363.0 2.0 fusion.43
  365.7 2.2 fusion.19
  367.9 30.7 %all_gather.40 = f32[7,4096]{1,0:T(8,128)S(1)} all-gather(f32[7,128]{1,0:T(8,128)S(1)} %pad_maximum_fusion.2), channel_id=1, replica_groups=mesh['grp'=8,'sub'=32] {'sub'}, dimensions={1}, use_global_device_ids=true | all-gather | bytes 118272 | tf_op jit(solution)/shard_map/all_gather | solution.py:91
  398.6 2.0 fusion.46
  401.3 2.2 fusion.21
  403.5 33.4 %all_gather.41 = f32[7,4096]{1,0:T(8,128)S(1)} all-gather(f32[7,128]{1,0:T(8,128)S(1)} %pad_maximum_fusion.1), channel_id=1, replica_groups=mesh['grp'=8,'sub'=32] {'sub'}, dimensions={1}, use_global_device_ids=true | all-gather | bytes 118272 | tf_op jit(solution)/shard_map/all_gather | solution.py:91
  437.0 2.0 fusion.49
  439.6 2.2 fusion.23
  441.8 31.1 %all_gather.42 = f32[7,4096]{1,0:T(8,128)S(1)} all-gather(f32[7,128]{1,0:T(8,128)S(1)} %pad_maximum_fusion), channel_id=1, replica_groups=mesh['grp'=8,'sub'=32] {'sub'}, dimensions={1}, use_global_device_ids=true | all-gather | bytes 118272 | tf_op jit(solution)/shard_map/all_gather | solution.py:91
  473.0 2.0 fusion.52
  475.6 2.2 fusion.25
  477.9 36.5 %all_gather.43 = f32[4,4096]{1,0:T(4,128)S(1)} all-gather(f32[4,128]{1,0:T(4,128)S(1)} %pad_maximum_fusion.9), channel_id=1, replica_groups=mesh['grp'=8,'sub'=32] {'sub'}, dimensions={1}, use_global_device_ids=true | all-gather | bytes 67584 | tf_op jit(solution)/shard_map/all_gather | solution.py:79
  514.4 8.5 %while.9 = (s32[]{:T(128)}, f32[4,3,128]{2,1,0:T(4,128)S(1)}, f32[3,4096]{1,0:T(4,128)S(1)}, f32[4,3,128]{2,1,0:T(4,128)S(1)}, f32[1,4096]{1,0:T(1,128)S(1)}, /*index=5*/s32[]{:T(128)}) while((s32[]{:T(128)}, f32[4,3,128]{2,1,0:T(4,128)S(1)}, f32[3,4096]{1,0:T(4,128)S(1)}, f32[4,3,128]{2,1,0:T(4,128)S(1)}, f32[1,4096]{1,0:T(1,128)S(1)}, ...), condition=%wide.region_45.46_spmd, body=%wide.region_42.45_spmd.sunk | while | flops 11009666 | bytes 8515149 | solution.py:34
  523.0 8.5 %while.11 = (s32[]{:T(128)}, f32[4,3,128]{2,1,0:T(4,128)S(1)}, f32[3,4096]{1,0:T(4,128)S(1)}, f32[4,3,128]{2,1,0:T(4,128)S(1)}, f32[1,4096]{1,0:T(1,128)S(1)}, /*index=5*/s32[]{:T(128)}) while((s32[]{:T(128)}, f32[4,3,128]{2,1,0:T(4,128)S(1)}, f32[3,4096]{1,0:T(4,128)S(1)}, f32[4,3,128]{2,1,0:T(4,128)S(1)}, f32[1,4096]{1,0:T(1,128)S(1)}, ...), condition=%wide.region_54.55_spmd, body=%wide.region_51.54_spmd.sunk | while | flops 11009666 | bytes 8515149 | solution.py:34
  532.1 10.4 %while.10 = (s32[]{:T(128)}, f32[4,3,1024]{2,1,0:T(4,128)S(1)}, f32[3,512]{1,0:T(4,128)S(1)}, f32[4,3,1024]{2,1,0:T(4,128)S(1)}, f32[512]{0:T(512)S(1)}, /*index=5*/s32[]{:T(128)}) while((s32[]{:T(128)}, f32[4,3,1024]{2,1,0:T(4,128)S(1)}, f32[3,512]{1,0:T(4,128)S(1)}, f32[4,3,1024]{2,1,0:T(4,128)S(1)}, f32[512]{0:T(512)S(1)}, ...), condition=%wide.region_49.50_spmd, body=%wide.region_46.49_spmd.sunk | while | flops 11006978 | bytes 8497229 | solution.py:34
  533.4 1.2 fusion.75
  534.7 0.9 fusion.74
  536.0 1.2 fusion.75
  538.6 1.2 fusion.75
  541.2 1.2 fusion.75
  542.5 171.9 %psum.15 = f32[3,4096]{1,0:T(4,128)S(1)} all-reduce(f32[3,4096]{1,0:T(4,128)S(1)} %bitcast.92), channel_id=1, replica_groups=mesh['grp'=8,'sub'=32] {'grp','sub'}, use_global_device_ids=true, to_apply=%region_50.51 | all-reduce | flops 12288 | bytes 98304 | tf_op jit(solution)/shard_map/psum | solution.py:82
  (150 shorter events, 32.9 us)
Async XLA Ops:
  43.2 102.1 %copy-start.6 = (f32[3,128]{1,0:T(4,128)S(1)}, f32[3,128]{1,0:T(4,128)}, u32[]{:S(2)}) copy-start(f32[3,128]{1,0:T(4,128)} %param.16) | copy-start | bytes 4612
  43.2 102.1 %copy-start.3 = (f32[3,128]{1,0:T(4,128)S(1)}, f32[3,128]{1,0:T(4,128)}, u32[]{:S(2)}) copy-start(f32[3,128]{1,0:T(4,128)} %param.15) | copy-start | bytes 4612
  44.9 0.7 copy-start
  48.6 0.7 copy-start
  52.2 0.7 copy-start
  55.8 0.7 copy-start
  475.6 38.8 %copy-start.1 = (f32[3,512]{1,0:T(4,128)S(1)}, f32[3,512]{1,0:T(4,128)}, u32[]{:S(2)}) copy-start(f32[3,512]{1,0:T(4,128)} %get-tuple-element.607) | copy-start | bytes 18436
  477.8 36.6 %copy-start.5 = (f32[3,128]{1,0:T(4,128)}, f32[3,128]{1,0:T(4,128)S(1)}, u32[]{:S(2)}) copy-start(f32[3,128]{1,0:T(4,128)S(1)} %multiply_add_fusion.2) | copy-start | bytes 4612
  514.4 8.5 %copy-start.4 = (f32[3,512]{1,0:T(4,128)S(1)}, f32[3,512]{1,0:T(4,128)}, u32[]{:S(2)}) copy-start(f32[3,512]{1,0:T(4,128)} %param.19) | copy-start | bytes 18436
  542.5 172.5 %copy-start.2 = (f32[3,512]{1,0:T(4,128)}, f32[3,512]{1,0:T(4,128)S(1)}, u32[]{:S(2)}) copy-start(f32[3,512]{1,0:T(4,128)S(1)} %get-tuple-element.610) | copy-start | bytes 18436
where the time goes:
time: 725 us; the launch traced here: 715 us
  blocking collectives  625 us (86%)
  other arithmetic  86 us (12%)
    all_gather x9, blocking collectives, evaluate(): source_piece = lax.all_gather(sources, 'sub', axis=1, tiled=True)  288 us
    psum x2, blocking collectives, kick(): summed = lax.psum(partial_value, ('grp', 'sub'))  259 us
    all_gather x2, blocking collectives, kick(): gathered = lax.all_gather(stacked, 'sub', axis=1, tiled=True)  76.9 us
    reduce_sum x8, other arithmetic, rates_one_tile(): jnp.sum((closing - radial[None] * separation) * weight[None], axis=2)  17.5 us
    reduce_sum x16, other arithmetic, field_one_tile(): distance = jnp.sum(separation * separation, axis=0) + soften  17.3 us
    reduce_sum x16, other arithmetic, field_one_tile(): return jnp.sum(separation * weight[None], axis=2)  16.5 us
    reduce_sum x8, other arithmetic, rates_one_tile(): radial = 3.0 * jnp.sum(separation * closing, axis=0) / distance  16.4 us

commit v1 on v0

--- a/solution.py
+++ b/solution.py
@@ -8,6 +8,11 @@
 bridge_soft = 0.01
 cluster_soft = 0.0025
 tile_limit = 524288
+
+
+def by_each_axis(x, inner_axis, outer_axis):
+    half = lax.psum(x, inner_axis)
+    return lax.psum(half, outer_axis)
 
 
 def pick_block(target_count, source_count):
@@ -79,7 +84,7 @@
         gathered = lax.all_gather(stacked, "sub", axis=1, tiled=True)
         galaxy_push = field(body_positions, gathered[:3], gathered[3], bridge_soft)
         partial_value = field(gathered[:3], body_positions, body_mass, bridge_soft)
-        summed = lax.psum(partial_value, ("grp", "sub"))
+        summed = by_each_axis(partial_value, "sub", "grp")
         cluster_pull = lax.dynamic_slice_in_dim(
             summed, lax.axis_index("sub") * star_count, star_count, 1
         )

time: 725 us -> 902 us (1.24)
  blocking collectives: 625 us -> 802 us
    psum x2 -> x4, blocking collectives: 259 us -> 437 us  [the longest x2 225 us: by_each_axis(): half = lax.psum(x, inner_axis)]
where the time goes in v1:
time: 902 us; the launch traced here: 893 us
  blocking collectives  802 us (89%)
  other arithmetic  86 us (10%)
    all_gather x9, blocking collectives, evaluate(): source_piece = lax.all_gather(sources, 'sub', axis=1, tiled=True)  288 us
    psum x2, blocking collectives, by_each_axis(): half = lax.psum(x, inner_axis)  225 us
    psum x2, blocking collectives, by_each_axis(): return lax.psum(half, outer_axis)  212 us
    all_gather x2, blocking collectives, kick(): gathered = lax.all_gather(stacked, 'sub', axis=1, tiled=True)  76.4 us

profile of v1, /device:TPU:1, one launch (start us, length us, event | category | flops | bytes accessed | tf_op | source)
XLA Modules:
  0.0 892.7 jit_solution(12041371922638758788)
XLA Ops:
  2.0 40.5 %all_gather.33 = f32[4,4096]{1,0:T(4,128)S(1)} all-gather(f32[4,128]{1,0:T(4,128)S(1)} %pad_maximum_fusion.10), channel_id=1, replica_groups=mesh['grp'=8,'sub'=32] {'sub'}, dimensions={1}, use_global_device_ids=true | all-gather | bytes 67584 | tf_op jit(solution)/shard_map/all_gather | solution.py:84
  43.3 14.5 %while.8 = (s32[]{:T(128)}, f32[4,3,1024]{2,1,0:T(4,128)S(1)}, f32[3,512]{1,0:T(4,128)}, f32[4,3,1024]{2,1,0:T(4,128)S(1)}, f32[512]{0:T(512)S(1)}, /*index=5*/s32[]{:T(128)}) while((s32[]{:T(128)}, f32[4,3,1024]{2,1,0:T(4,128)S(1)}, f32[3,512]{1,0:T(4,128)}, f32[4,3,1024]{2,1,0:T(4,128)S(1)}, f32[512]{0:T(512)S(1)}, ...), condition=%wide.region_4.5_spmd, body=%wide.region_1.4_spmd.sunk | while | flops 11006978 | bytes 8521833 | solution.py:39
  43.3 1.6 fusion.70
  45.6 1.2 fusion.71
  46.9 1.6 fusion.70
  49.3 1.2 fusion.71
  50.5 1.6 fusion.70
  52.9 1.2 fusion.71
  54.2 1.6 fusion.70
  57.8 112.9 %psum.28 = f32[3,4096]{1,0:T(4,128)S(1)} all-reduce(f32[3,4096]{1,0:T(4,128)S(1)} %bitcast.93), channel_id=1, replica_groups=mesh['grp'=8,'sub'=32] {'sub'}, use_global_device_ids=true, to_apply=%region_5.6 | all-reduce | flops 12288 | bytes 98304 | tf_op jit(solution)/shard_map/psum | solution.py:14
  170.7 61.4 %psum.29 = f32[3,4096]{1,0:T(4,128)S(1)} all-reduce(f32[3,4096]{1,0:T(4,128)S(1)} %psum.28), channel_id=1, replica_groups=mesh['grp'=8,'sub'=32] {'grp'}, use_global_device_ids=true, to_apply=%region_6.7 | all-reduce | flops 12288 | bytes 98304 | tf_op jit(solution)/shard_map/psum | solution.py:15
  232.2 30.2 %all_gather.34 = f32[7,4096]{1,0:T(8,128)S(1)} all-gather(f32[7,128]{1,0:T(8,128)S(1)} %pad_maximum_fusion.8), channel_id=1, replica_groups=mesh['grp'=8,'sub'=32] {'sub'}, dimensions={1}, use_global_device_ids=true | all-gather | bytes 118272 | tf_op jit(solution)/shard_map/all_gather | solution.py:96
  262.4 1.9 fusion.26
  264.9 2.1 fusion.27
  267.1 33.0 %all_gather.35 = f32[7,4096]{1,0:T(8,128)S(1)} all-gather(f32[7,128]{1,0:T(8,128)S(1)} %pad_maximum_fusion.7), channel_id=1, replica_groups=mesh['grp'=8,'sub'=32] {'sub'}, dimensions={1}, use_global_device_ids=true | all-gather | bytes 118272 | tf_op jit(solution)/shard_map/all_gather | solution.py:96
  300.2 2.0 fusion.31
  302.8 2.2 fusion.11
  305.1 31.8 %all_gather.36 = f32[7,4096]{1,0:T(8,128)S(1)} all-gather(f32[7,128]{1,0:T(8,128)S(1)} %pad_maximum_fusion.6), channel_id=1, replica_groups=mesh['grp'=8,'sub'=32] {'sub'}, dimensions={1}, use_global_device_ids=true | all-gather | bytes 118272 | tf_op jit(solution)/shard_map/all_gather | solution.py:96
  336.9 2.0 fusion.34
  339.5 2.2 fusion.13
  341.8 33.4 %all_gather.37 = f32[7,4096]{1,0:T(8,128)S(1)} all-gather(f32[7,128]{1,0:T(8,128)S(1)} %pad_maximum_fusion.5), channel_id=1, replica_groups=mesh['grp'=8,'sub'=32] {'sub'}, dimensions={1}, use_global_device_ids=true | all-gather | bytes 118272 | tf_op jit(solution)/shard_map/all_gather | solution.py:96
  375.2 2.0 fusion.37
  377.9 2.2 fusion.15
  380.1 30.8 %all_gather.38 = f32[7,4096]{1,0:T(8,128)S(1)} all-gather(f32[7,128]{1,0:T(8,128)S(1)} %pad_maximum_fusion.4), channel_id=1, replica_groups=mesh['grp'=8,'sub'=32] {'sub'}, dimensions={1}, use_global_device_ids=true | all-gather | bytes 118272 | tf_op jit(solution)/shard_map/all_gather | solution.py:96
  411.0 2.0 fusion.40
  413.6 2.2 fusion.17
  415.9 33.1 %all_gather.39 = f32[7,4096]{1,0:T(8,128)S(1)} all-gather(f32[7,128]{1,0:T(8,128)S(1)} %pad_maximum_fusion.3), channel_id=1, replica_groups=mesh['grp'=8,'sub'=32] {'sub'}, dimensions={1}, use_global_device_ids=true | all-gather | bytes 118272 | tf_op jit(solution)/shard_map/all_gather | solution.py:96
  449.0 2.0 fusion.43
  451.7 2.2 fusion.19
  453.9 30.5 %all_gather.40 = f32[7,4096]{1,0:T(8,128)S(1)} all-gather(f32[7,128]{1,0:T(8,128)S(1)} %pad_maximum_fusion.2), channel_id=1, replica_groups=mesh['grp'=8,'sub'=32] {'sub'}, dimensions={1}, use_global_device_ids=true | all-gather | bytes 118272 | tf_op jit(solution)/shard_map/all_gather | solution.py:96
  484.4 2.0 fusion.46
  487.0 2.2 fusion.21
  489.3 33.7 %all_gather.41 = f32[7,4096]{1,0:T(8,128)S(1)} all-gather(f32[7,128]{1,0:T(8,128)S(1)} %pad_maximum_fusion.1), channel_id=1, replica_groups=mesh['grp'=8,'sub'=32] {'sub'}, dimensions={1}, use_global_device_ids=true | all-gather | bytes 118272 | tf_op jit(solution)/shard_map/all_gather | solution.py:96
  523.0 2.0 fusion.49
  525.6 2.2 fusion.23
  527.8 31.8 %all_gather.42 = f32[7,4096]{1,0:T(8,128)S(1)} all-gather(f32[7,128]{1,0:T(8,128)S(1)} %pad_maximum_fusion), channel_id=1, replica_groups=mesh['grp'=8,'sub'=32] {'sub'}, dimensions={1}, use_global_device_ids=true | all-gather | bytes 118272 | tf_op jit(solution)/shard_map/all_gather | solution.py:96
  559.6 2.0 fusion.52
  562.3 2.2 fusion.25
  564.5 35.9 %all_gather.43 = f32[4,4096]{1,0:T(4,128)S(1)} all-gather(f32[4,128]{1,0:T(4,128)S(1)} %pad_maximum_fusion.9), channel_id=1, replica_groups=mesh['grp'=8,'sub'=32] {'sub'}, dimensions={1}, use_global_device_ids=true | all-gather | bytes 67584 | tf_op jit(solution)/shard_map/all_gather | solution.py:84
  600.6 8.5 while.9
  609.1 8.5 while.11
  618.2 10.4 %while.10 = (s32[]{:T(128)}, f32[4,3,1024]{2,1,0:T(4,128)S(1)}, f32[3,512]{1,0:T(4,128)S(1)}, f32[4,3,1024]{2,1,0:T(4,128)S(1)}, f32[512]{0:T(512)S(1)}, /*index=5*/s32[]{:T(128)}) while((s32[]{:T(128)}, f32[4,3,1024]{2,1,0:T(4,128)S(1)}, f32[3,512]{1,0:T(4,128)S(1)}, f32[4,3,1024]{2,1,0:T(4,128)S(1)}, f32[512]{0:T(512)S(1)}, ...), condition=%wide.region_50.51_spmd, body=%wide.region_47.50_spmd.sunk | while | flops 11006978 | bytes 8497229 | solution.py:39
  619.6 1.2 fusion.75
  622.2 1.2 fusion.75
  624.8 1.2 fusion.75
  627.3 1.2 fusion.75
  628.6 112.2 %psum.30 = f32[3,4096]{1,0:T(4,128)S(1)} all-reduce(f32[3,4096]{1,0:T(4,128)S(1)} %bitcast.92), channel_id=1, replica_groups=mesh['grp'=8,'sub'=32] {'sub'}, use_global_device_ids=true, to_apply=%region_51.52 | all-reduce | flops 12288 | bytes 98304 | tf_op jit(solution)/shard_map/psum | solution.py:14
  740.8 150.9 %psum.31 = f32[3,4096]{1,0:T(4,128)S(1)} all-reduce(f32[3,4096]{1,0:T(4,128)S(1)} %psum.30), channel_id=1, replica_groups=mesh['grp'=8,'sub'=32] {'grp'}, use_global_device_ids=true, to_apply=%region_52.53 | all-reduce | flops 12288 | bytes 98304 | tf_op jit(solution)/shard_map/psum | solution.py:15
  (152 shorter events, 35.1 us)
Async XLA Ops:
  43.2 188.9 %copy-start.6 = (f32[3,128]{1,0:T(4,128)S(1)}, f32[3,128]{1,0:T(4,128)}, u32[]{:S(2)}) copy-start(f32[3,128]{1,0:T(4,128)} %param.16) | copy-start | bytes 4612
  43.2 188.9 %copy-start.3 = (f32[3,128]{1,0:T(4,128)S(1)}, f32[3,128]{1,0:T(4,128)}, u32[]{:S(2)}) copy-start(f32[3,128]{1,0:T(4,128)} %param.15) | copy-start | bytes 4612
  44.9 0.7 copy-start
  48.6 0.7 copy-start
  52.2 0.7 copy-start
  55.8 0.7 copy-start
  562.3 38.3 %copy-start.1 = (f32[3,512]{1,0:T(4,128)S(1)}, f32[3,512]{1,0:T(4,128)}, u32[]{:S(2)}) copy-start(f32[3,512]{1,0:T(4,128)} %get-tuple-element.607) | copy-start | bytes 18436
  564.5 36.1 %copy-start.5 = (f32[3,128]{1,0:T(4,128)}, f32[3,128]{1,0:T(4,128)S(1)}, u32[]{:S(2)}) copy-start(f32[3,128]{1,0:T(4,128)S(1)} %multiply_add_fusion.2) | copy-start | bytes 4612
  600.5 8.5 copy-start.4
  628.6 263.7 %copy-start.2 = (f32[3,512]{1,0:T(4,128)}, f32[3,512]{1,0:T(4,128)S(1)}, u32[]{:S(2)}) copy-start(f32[3,512]{1,0:T(4,128)S(1)} %get-tuple-element.610) | copy-start | bytes 18436
